TPU v7x, 32 devices: a whole 2x2x4 slice. The times are simulated.
32 devices in a mesh: seq: 8 (over y, x, core), tp: 4 (over z).
Axes of the slice: x: 2, y: 2, z: 4, core: 2. Of those that a mesh axis runs over, the one named last changes fastest.
Arguments:
- grad_out: bfloat16 [1024, 8192], P('seq', 'tp'), may hold values from -6 to 6
- resid_in: bfloat16 [1024, 8192], P('seq', 'tp'), may hold values from -6 to 6
- down_weight: bfloat16 [28672, 8192], P('seq', 'tp'), may hold values from -0.03125 to 0.03125
- hidden_clean: bfloat16 [28672, 512], P('seq', 'tp'), may hold values from -6 to 6
- hidden_corrupt: bfloat16 [28672, 512], P('seq', 'tp'), may hold values from -6 to 6
- patched: int32 [14336], replicated, may hold values from 0 to 28671, as said below
Outputs:
- resid_scores: float32 [1024], P('seq')
- token_scores: float32 [512], P('tp')
- neuron_scores: float32 [28672], P('seq')
Inputs may be any that keep to these rules, and one draw needn't show every extreme that they name: `patched`: 14336 distinct hidden-unit indices.
All inputs are finite; a program needn't handle non-finite values.
Results may differ from a plain program's by a relative error of at most 0.0046.
Values may be sent and summed in bfloat16 or wider, within the bound.
A program may use at most 128 MiB of HBM per device.

v0:
```python
import math
import jax
import jax.numpy as jnp
from jax import lax
from jax.sharding import PartitionSpec as P


def from_behind(value, axis, steps):
    count = lax.axis_size(axis)
    pairs = [(source, (source + steps) % count) for source in range(count)]
    return lax.ppermute(value, axis, pairs)


def patch_mask(patched, unit_rows):
    lanes = math.gcd(unit_rows, 128)
    groups = unit_rows // lanes
    local = patched - lax.axis_index("seq") * unit_rows
    high = local[None, :] // lanes == jnp.arange(groups, dtype=jnp.int32)[:, None]
    high = high & (local >= 0)[None, :]
    low = (local % lanes)[:, None] == jnp.arange(lanes, dtype=jnp.int32)[None, :]
    counts = lax.dot_general(
        high.astype(jnp.bfloat16),
        low.astype(jnp.bfloat16),
        (((1,), (0,)), ((), ())),
        preferred_element_type=jnp.float32,
    )
    return counts.reshape(unit_rows)


def shards(grad_out, resid_in, down_weight, hidden_clean, hidden_corrupt, patched):
    seq_count = lax.axis_size("seq")
    tp_count = lax.axis_size("tp")
    pair_count = seq_count // 2
    half_rows = grad_out.shape[0] // 2
    unit_rows = down_weight.shape[0]
    model_width = resid_in.shape[1] * tp_count
    hidden_diff = (hidden_clean.astype(jnp.float32) - hidden_corrupt.astype(jnp.float32)).astype(
        jnp.bfloat16
    )
    diff_all = lax.all_gather(hidden_diff, "tp", axis=0)
    in_upper = lax.axis_index("seq") // pair_count
    send_start = (1 - in_upper) * half_rows
    keep_start = in_upper * half_rows
    sent_grad = lax.dynamic_slice_in_dim(grad_out, send_start, half_rows, 0)
    partner_grad = from_behind(sent_grad, "seq", pair_count)
    partner_resid = from_behind(resid_in, "seq", pair_count)
    sign_factor = (1 - 2 * in_upper).astype(jnp.float32)
    resid_diff = sign_factor * (resid_in.astype(jnp.float32) - partner_resid.astype(jnp.float32))
    resid_part = jnp.sum(resid_diff * grad_out.astype(jnp.float32), axis=1)
    kept_grad = lax.dynamic_slice_in_dim(grad_out, keep_start, half_rows, 0)
    grad_mean = ((kept_grad.astype(jnp.float32) + partner_grad.astype(jnp.float32)) * 0.5).astype(
        jnp.bfloat16
    )
    grads = lax.all_gather(grad_mean, "seq", axis=0)
    width = grads.shape[-1]
    grads = grads.reshape(2, pair_count, half_rows, width).transpose(1, 0, 2, 3)
    grads = grads.reshape(-1, width)
    total_len = grads.shape[0]
    in_patch = patch_mask(patched, unit_rows)
    unit_grad = lax.dot_general(
        down_weight, grads, (((1,), (1,)), ((), ())), preferred_element_type=jnp.float32
    )
    local_len = total_len // tp_count
    token_parts = []
    unit_part = 0.0
    for block in range(tp_count):
        part = unit_grad[:, block * local_len : (block + 1) * local_len]
        product = diff_all[block].astype(jnp.float32) * part
        token_parts.append(jnp.sum(product * in_patch[:, None], axis=0))
        unit_part = unit_part + jnp.sum(product, axis=1)
    token_part = jnp.stack(token_parts)
    token_total = lax.psum(token_part, ("seq", "tp"))
    token_mine = lax.dynamic_index_in_dim(token_total, lax.axis_index("tp"), 0, keepdims=False)
    token_scores = token_mine / math.sqrt(patched.shape[0])
    unit_total, resid_total = lax.psum((unit_part, resid_part), "tp")
    neuron_scores = unit_total / math.sqrt(total_len)
    resid_scores = resid_total / math.sqrt(model_width)
    return (resid_scores, token_scores, neuron_scores)


def solution(mesh):
    in_specs = (P("seq", "tp"), P("seq", "tp"), P("seq", "tp"), P("seq", "tp"), P("seq", "tp"), P())
    out_specs = (P("seq"), P("tp"), P("seq"))
    return jax.shard_map(shards, mesh=mesh, in_specs=in_specs, out_specs=out_specs, check_vma=False)
```

profile of v0, /device:TPU:10, one launch (start us, length us, event | category | flops | bytes accessed | tf_op | source)
XLA Modules:
  0.0 192.9 jit_solution(12017848095058334556)
XLA Ops:
  7.3 1.1 constant_dynamic-slice_fusion.1
  8.3 1.6 collective-permute-start.1
  9.9 6.5 %collective-permute-done.1 = bf16[64,2048]{1,0:T(8,128)(2,1)S(1)} collective-permute-done((bf16[64,2048]{1,0:T(8,128)(2,1)S(1)}, bf16[64,2048]{1,0:T(8,128)(2,1)S(1)}, u32[]{:S(2)}, u32[]{:S(2)}) %collective-permute-start.1) | collective-permute-done | bytes 262176 | tf_op jit(solution)/shard_map/ppermute | solution.py:11
  16.5 1.8 multiply_convert_fusion
  18.2 0.0 all-gather.5.cloned.1.call-start
  18.3 1.6 collective-permute-start
  19.9 0.5 copy.14
  20.4 0.5 copy.13
  20.9 1.1 subtract_convert_fusion
  22.1 0.1 add_select_fusion.1
  22.2 0.3 fusion.22
  22.6 2.1 %fusion.8 = f32[3584]{0:T(1024)S(1)} fusion(s32[14336]{0:T(1024)S(1)} %get-tuple-element.18, pred[28,14336]{1,0:T(8,128)(4,1)S(1)} %fusion.22), kind=kOutput, calls=%fused_computation.19 | convolution fusion | flops 104595456 | bytes 473088 | tf_op jit(solution)/shard_map/dot_general | solution.py:21
  24.7 9.5 %collective-permute-done = bf16[128,2048]{1,0:T(8,128)(2,1)S(1)} collective-permute-done((bf16[128,2048]{1,0:T(8,128)(2,1)}, bf16[128,2048]{1,0:T(8,128)(2,1)S(1)}, u32[]{:S(2)}, u32[]{:S(2)}) %collective-permute-start) | collective-permute-done | bytes 524320 | tf_op jit(solution)/shard_map/ppermute | solution.py:11
  34.2 0.3 multiply_reduce_fusion.4
  34.5 14.7 %all-gather.7.cloned.1.call-done = bf16[512,2048]{1,0:T(8,128)(2,1)} async-done(((bf16[64,2048]{1,0:T(8,128)(2,1)}), bf16[512,2048]{1,0:T(8,128)(2,1)}) %all-gather.7.cloned.1.call-update) | async-done | bytes 2097168 | tf_op jit(solution)/shard_map/all_gather | solution.py:54
  49.2 1.7 copy.15
  51.0 13.1 %convolution_bitcast_fusion = f32[3584,512]{0,1:T(8,128)} fusion(bf16[512,2048]{1,0:T(8,128)(2,1)S(1)} %bitcast.20, bf16[3584,2048]{1,0:T(8,128)(2,1)} %param.8), kind=kOutput, calls=%fused_computation.2 | convolution fusion | flops 7516192768 | bytes 24117248 | tf_op jit(solution)/shard_map/dot_general | solution.py:60
  64.1 56.5 %all-gather.5.cloned.1.call-done = bf16[14336,128]{0,1:T(8,128)(2,1)} async-done(((bf16[3584,128]{0,1:T(8,128)(2,1)}), bf16[14336,128]{0,1:T(8,128)(2,1)}) %all-gather.5.cloned.1.call-update) | async-done | bytes 3670032 | tf_op jit(solution)/shard_map/all_gather | solution.py:40
  120.5 4.9 %fusion.5 = (f32[3584]{0:T(1024)S(1)}, f32[3584]{0:T(1024)S(1)}, f32[3584]{0:T(1024)S(1)}, f32[3584]{0:T(1024)S(1)}, f32[128]{0:T(128)S(1)}, /*index=5*/f32[128]{0:T(128)S(1)}, f32[128]{0:T(128)S(1)}, f32[128]{0:T(128)S(1)}) fusion(f32[3584,512]{0,1:T(8,128)} %convolution_bitcast_fusion, bf16[14336,128]{0,1:T(8,128)(2,1)} %all-gather.5.cloned.1.call-done, ...), kind=kLoop, calls=%fused_computation.16 | loop fusion | flops 9160192 | bytes 11083776 | tf_op jit(solution)/shard_map/reduce_sum | solution.py:70
  125.4 16.7 %all-reduce = (f32[128]{0:T(128)S(1)}, f32[3584]{0:T(1024)S(1)}) all-reduce(f32[128]{0:T(128)S(1)} %multiply_reduce_fusion.4, f32[3584]{0:T(1024)S(1)} %add_add_fusion), channel_id=1, replica_groups=mesh['seq'=8,'tp'=4] {'tp'}, use_global_device_ids=true, to_apply=%region_1.2 | all-reduce | flops 3712 | bytes 29696 | tf_op jit(solution)/shard_map/psum | solution.py:75
  142.1 0.5 broadcast_multiply_fusion.1
  142.7 42.3 %psum.22 = f32[4,128]{1,0:T(4,128)S(1)} all-reduce(f32[4,128]{1,0:T(4,128)S(1)} %pad_maximum_fusion), channel_id=1, replica_groups=mesh['seq'=8,'tp'=4] {'seq','tp'}, use_global_device_ids=true, to_apply=%region_6.7 | all-reduce | flops 512 | bytes 4096 | tf_op jit(solution)/shard_map/psum | solution.py:72
  185.0 0.6 broadcast_multiply_fusion
  185.6 0.5 fusion.16
  (16 shorter events, 0.1 us)
Async XLA Ops:
  7.2 12.7 %copy-start.1 = (bf16[3584,128]{1,0:T(8,128)(2,1)S(1)}, bf16[3584,128]{1,0:T(8,128)(2,1)}, u32[]{:S(2)}) copy-start(bf16[3584,128]{1,0:T(8,128)(2,1)} %param.10) | copy-start | bytes 2752516
  7.2 13.2 %copy-start.2 = (bf16[3584,128]{1,0:T(8,128)(2,1)S(1)}, bf16[3584,128]{1,0:T(8,128)(2,1)}, u32[]{:S(2)}) copy-start(bf16[3584,128]{1,0:T(8,128)(2,1)} %param.9) | copy-start | bytes 2752516
  7.2 42.0 %all-gather.7.cloned.1.call-start = ((), (), s32[]{:S(2)}) async-start(), calls=%async_computation.1 | async-start | bytes 2359296 | tf_op jit(solution)/shard_map/all_gather | solution.py:54
  8.3 8.1 %collective-permute-start.1 = (bf16[64,2048]{1,0:T(8,128)(2,1)S(1)}, bf16[64,2048]{1,0:T(8,128)(2,1)S(1)}, u32[]{:S(2)}, u32[]{:S(2)}) collective-permute-start(bf16[64,2048]{1,0:T(8,128)(2,1)S(1)} %constant_dynamic-slice_fusion.1), channel_id=1, source_target_pairs={{0,16},{4,20},{8,24},{12,28},{16,0},{20,4},{24,8},{28,12},{1,17},{... | collective-permute-start | bytes 786440 | tf_op jit(solution)/shard_map/ppermute | solution.py:11
  18.2 102.3 %all-gather.5.cloned.1.call-start = ((), (), s32[]{:S(2)}) async-start(), calls=%async_computation | async-start | bytes 4587520 | tf_op jit(solution)/shard_map/all_gather | solution.py:40
  18.3 15.9 %collective-permute-start = (bf16[128,2048]{1,0:T(8,128)(2,1)}, bf16[128,2048]{1,0:T(8,128)(2,1)S(1)}, u32[]{:S(2)}, u32[]{:S(2)}) collective-permute-start(bf16[128,2048]{1,0:T(8,128)(2,1)} %param.7), channel_id=1, source_target_pairs={{0,16},{4,20},{8,24},{12,28},{16,0},{20,4},{24,8},{28,12},{1,17},{... | collective-permute-start | bytes 1572872 | tf_op jit(solution)/shard_map/ppermute | solution.py:11
  20.9 1.2 copy-start.4
  22.2 12.0 %copy-start = (bf16[128,2048]{1,0:T(8,128)(2,1)S(1)}, bf16[128,2048]{1,0:T(8,128)(2,1)}, u32[]{:S(2)}) copy-start(bf16[128,2048]{1,0:T(8,128)(2,1)} %param.6) | copy-start | bytes 1572868
  22.2 11.9 %copy-start.3 = (bf16[128,2048]{1,0:T(8,128)(2,1)S(1)}, bf16[128,2048]{1,0:T(8,128)(2,1)}, u32[]{:S(2)}) copy-start(bf16[128,2048]{1,0:T(8,128)(2,1)} %param.7) | copy-start | bytes 1572868
Sparse Core Ops, SparseCore 0:
  18.4 30.8 all-gather.6
  50.8 69.7 all-gather.4
where the time goes:
time: 193 us
  waiting for transfers between devices  87.2 us (45%)
  blocking collectives  59 us (31%)
  matrix products  15.2 us (8%)
  between operations  14.2 us (7%)
  other arithmetic  10.2 us (5%)
  local copies, waits for them, and re-layouts  3.87 us (2%)
  starting transfers between devices  3.25 us (2%)
    all_gather x1, waiting for transfers between devices, shards(): diff_all = lax.all_gather(hidden_diff, 'tp', axis=0)  56.5 us
    psum x1, blocking collectives, shards(): token_total = lax.psum(token_part, ('seq', 'tp'))  42.3 us
    psum x1, blocking collectives, shards(): unit_total, resid_total = lax.psum((unit_part, resid_part), 'tp')  16.7 us
    ppermute x2, waiting for transfers between devices, from_behind(): return lax.ppermute(value, axis, pairs)  16 us
    all_gather x1, waiting for transfers between devices, shards(): grads = lax.all_gather(grad_mean, 'seq', axis=0)  14.7 us
    dot_general x1, matrix products, shards(): lax.dot_general(down_weight, grads, (((1,), (1,)), ((), ())), preferred_e...  13.1 us
    reduce_sum x1, other arithmetic, shards(): unit_part = unit_part + jnp.sum(product, axis=1)  4.87 us
  transfers between devices with their start and end apart: 4, of which 4 were waited for; matrix products, arithmetic and copies ran while one was open for 10% of the time, Pallas kernels for 0%

commit v1 on v0

--- a/solution.py
+++ b/solution.py
@@ -69,7 +69,9 @@
         token_parts.append(jnp.sum(product * in_patch[:, None], axis=0))
         unit_part = unit_part + jnp.sum(product, axis=1)
     token_part = jnp.stack(token_parts)
-    token_total = lax.psum(token_part, ("seq", "tp"))
+    token_total = token_part
+    for p in ("tp", "seq"):
+        token_total = lax.psum(token_total, p)
     token_mine = lax.dynamic_index_in_dim(token_total, lax.axis_index("tp"), 0, keepdims=False)
     token_scores = token_mine / math.sqrt(patched.shape[0])
     unit_total, resid_total = lax.psum((unit_part, resid_part), "tp")

time: 193 us -> 166 us (0.86)
  the two profiles are of different devices: /device:TPU:10 before, /device:TPU:0 now
where the time goes in v1:
time: 166 us
  waiting for transfers between devices  89.5 us (54%)
  blocking collectives  28.1 us (17%)
  matrix products  15.2 us (9%)
  between operations  14.2 us (9%)
  other arithmetic  10.2 us (6%)
  starting transfers between devices  4.92 us (3%)
  local copies, waits for them, and re-layouts  3.87 us (2%)
    all_gather x1, waiting for transfers between devices, shards(): diff_all = lax.all_gather(hidden_diff, 'tp', axis=0)  58.9 us
    psum x1, blocking collectives, shards(): unit_total, resid_total = lax.psum((unit_part, resid_part), 'tp')  16.3 us
    ppermute x2, waiting for transfers between devices, from_behind(): return lax.ppermute(value, axis, pairs)  15.9 us
    all_gather x1, waiting for transfers between devices, shards(): grads = lax.all_gather(grad_mean, 'seq', axis=0)  14.7 us
    dot_general x1, matrix products, shards(): lax.dot_general(down_weight, grads, (((1,), (1,)), ((), ())), preferred_e...  13.1 us
    psum x1, blocking collectives, shards(): token_total = lax.psum(token_total, p)  11.8 us
    reduce_sum x1, other arithmetic, shards(): unit_part = unit_part + jnp.sum(product, axis=1)  4.87 us
    ppermute x2, starting transfers between devices, from_behind(): return lax.ppermute(value, axis, pairs)  4.84 us
  transfers between devices with their start and end apart: 4, of which 4 were waited for; matrix products, arithmetic and copies ran while one was open for 12% of the time, Pallas kernels for 0%

profile of v1, /device:TPU:0, one launch (start us, length us, event | category | flops | bytes accessed | tf_op | source)
XLA Modules:
  0.0 166.0 jit_solution(5245824860959487487)
XLA Ops:
  7.3 1.1 constant_dynamic-slice_fusion.1
  8.3 3.0 %collective-permute-start.1 = (bf16[64,2048]{1,0:T(8,128)(2,1)S(1)}, bf16[64,2048]{1,0:T(8,128)(2,1)S(1)}, u32[]{:S(2)}, u32[]{:S(2)}) collective-permute-start(bf16[64,2048]{1,0:T(8,128)(2,1)S(1)} %constant_dynamic-slice_fusion.1), channel_id=1, source_target_pairs={{0,16},{4,20},{8,24},{12,28},{16,0},{20,4},{24,8},{28,12},{1,17},{... | collective-permute-start | bytes 786440 | tf_op jit(solution)/shard_map/ppermute | solution.py:11
  11.4 6.3 %collective-permute-done.1 = bf16[64,2048]{1,0:T(8,128)(2,1)S(1)} collective-permute-done((bf16[64,2048]{1,0:T(8,128)(2,1)S(1)}, bf16[64,2048]{1,0:T(8,128)(2,1)S(1)}, u32[]{:S(2)}, u32[]{:S(2)}) %collective-permute-start.1) | collective-permute-done | bytes 262176 | tf_op jit(solution)/shard_map/ppermute | solution.py:11
  17.7 1.8 %multiply_convert_fusion = bf16[64,2048]{1,0:T(8,128)(2,1)} fusion(bf16[64,2048]{1,0:T(8,128)(2,1)S(1)} %collective-permute-done.1, bf16[128,2048]{1,0:T(8,128)(2,1)} %param.6, s32[]{:T(128)S(6)} %select_n.28), kind=kLoop, calls=%fused_computation.23 | loop fusion | flops 655360 | bytes 786436 | tf_op jit(solution)/shard_map/convert_element_type | solution.py:51
  19.5 0.0 all-gather.5.cloned.1.call-start
  19.5 1.8 %collective-permute-start = (bf16[128,2048]{1,0:T(8,128)(2,1)}, bf16[128,2048]{1,0:T(8,128)(2,1)S(1)}, u32[]{:S(2)}, u32[]{:S(2)}) collective-permute-start(bf16[128,2048]{1,0:T(8,128)(2,1)} %param.7), channel_id=1, source_target_pairs={{0,16},{4,20},{8,24},{12,28},{16,0},{20,4},{24,8},{28,12},{1,17},{... | collective-permute-start | bytes 1572872 | tf_op jit(solution)/shard_map/ppermute | solution.py:11
  21.3 0.5 copy.14
  21.9 0.5 copy.13
  22.4 1.1 subtract_convert_fusion
  23.6 0.1 add_select_fusion.1
  23.7 0.3 fusion.22
  24.0 2.1 %fusion.8 = f32[3584]{0:T(1024)S(1)} fusion(s32[14336]{0:T(1024)S(1)} %get-tuple-element.19, pred[28,14336]{1,0:T(8,128)(4,1)S(1)} %fusion.22), kind=kOutput, calls=%fused_computation.19 | convolution fusion | flops 104595456 | bytes 473088 | tf_op jit(solution)/shard_map/dot_general | solution.py:21
  26.1 9.6 %collective-permute-done = bf16[128,2048]{1,0:T(8,128)(2,1)S(1)} collective-permute-done((bf16[128,2048]{1,0:T(8,128)(2,1)}, bf16[128,2048]{1,0:T(8,128)(2,1)S(1)}, u32[]{:S(2)}, u32[]{:S(2)}) %collective-permute-start) | collective-permute-done | bytes 524320 | tf_op jit(solution)/shard_map/ppermute | solution.py:11
  35.7 0.4 multiply_reduce_fusion.4
  36.1 14.7 %all-gather.7.cloned.1.call-done = bf16[512,2048]{1,0:T(8,128)(2,1)} async-done(((bf16[64,2048]{1,0:T(8,128)(2,1)}), bf16[512,2048]{1,0:T(8,128)(2,1)}) %all-gather.7.cloned.1.call-update) | async-done | bytes 2097168 | tf_op jit(solution)/shard_map/all_gather | solution.py:54
  50.8 1.7 %copy.15 = bf16[4,2,64,2048]{3,2,1,0:T(8,128)(2,1)S(1)} copy(bf16[4,2,64,2048]{3,2,0,1:T(8,128)(2,1)} %bitcast.19) | data formatting | bytes 4194304 | tf_op jit(solution)/shard_map/transpose | solution.py:56
  52.5 13.1 %convolution_bitcast_fusion = f32[3584,512]{0,1:T(8,128)} fusion(bf16[512,2048]{1,0:T(8,128)(2,1)S(1)} %bitcast.20, bf16[3584,2048]{1,0:T(8,128)(2,1)} %param.8), kind=kOutput, calls=%fused_computation.2 | convolution fusion | flops 7516192768 | bytes 24117248 | tf_op jit(solution)/shard_map/dot_general | solution.py:60
  65.6 58.9 %all-gather.5.cloned.1.call-done = bf16[14336,128]{0,1:T(8,128)(2,1)} async-done(((bf16[3584,128]{0,1:T(8,128)(2,1)}), bf16[14336,128]{0,1:T(8,128)(2,1)}) %all-gather.5.cloned.1.call-update) | async-done | bytes 3670032 | tf_op jit(solution)/shard_map/all_gather | solution.py:40
  124.5 4.9 %fusion.5 = (f32[3584]{0:T(1024)S(1)}, f32[3584]{0:T(1024)S(1)}, f32[3584]{0:T(1024)S(1)}, f32[3584]{0:T(1024)S(1)}, f32[128]{0:T(128)S(1)}, /*index=5*/f32[128]{0:T(128)S(1)}, f32[128]{0:T(128)S(1)}, f32[128]{0:T(128)S(1)}) fusion(f32[3584,512]{0,1:T(8,128)} %convolution_bitcast_fusion, bf16[14336,128]{0,1:T(8,128)(2,1)} %all-gather.5.cloned.1.call-done, ...), kind=kLoop, calls=%fused_computation.16 | loop fusion | flops 9160192 | bytes 11083776 | tf_op jit(solution)/shard_map/reduce_sum | solution.py:70
  129.4 16.3 %all-reduce = (f32[128]{0:T(128)S(1)}, f32[4,128]{1,0:T(4,128)S(1)}, f32[3584]{0:T(1024)S(1)}) all-reduce(f32[128]{0:T(128)S(1)} %multiply_reduce_fusion.4, f32[4,128]{1,0:T(4,128)S(1)} %pad_maximum_fusion, f32[3584]{0:T(1024)S(1)} %add_add_fusion), channel_id=1, replica_groups=mesh['seq'=8,'tp'=4] {'tp'}, use_global_device_ids=true, to_apply=%region_1.2 | all-reduce | flops 4224 | bytes 33792 | tf_op jit(solution)/shard_map/psum | solution.py:77
  145.7 0.5 broadcast_multiply_fusion.1
  146.2 11.8 %psum.30 = f32[4,128]{1,0:T(4,128)S(1)} all-reduce(f32[4,128]{1,0:T(4,128)S(1)} %get-tuple-element.16), channel_id=1, replica_groups=mesh['seq'=8,'tp'=4] {'seq'}, use_global_device_ids=true, to_apply=%region_7.8 | all-reduce | flops 512 | bytes 4096 | tf_op jit(solution)/shard_map/psum | solution.py:74
  158.0 0.6 broadcast_multiply_fusion
  158.6 0.5 fusion.16
  (16 shorter events, 0.1 us)
Async XLA Ops:
  7.2 14.2 %copy-start.1 = (bf16[3584,128]{1,0:T(8,128)(2,1)S(1)}, bf16[3584,128]{1,0:T(8,128)(2,1)}, u32[]{:S(2)}) copy-start(bf16[3584,128]{1,0:T(8,128)(2,1)} %param.10) | copy-start | bytes 2752516
  7.2 14.7 %copy-start.2 = (bf16[3584,128]{1,0:T(8,128)(2,1)S(1)}, bf16[3584,128]{1,0:T(8,128)(2,1)}, u32[]{:S(2)}) copy-start(bf16[3584,128]{1,0:T(8,128)(2,1)} %param.9) | copy-start | bytes 2752516
  7.2 43.6 %all-gather.7.cloned.1.call-start = ((), (), s32[]{:S(2)}) async-start(), calls=%async_computation.1 | async-start | bytes 2359296 | tf_op jit(solution)/shard_map/all_gather | solution.py:54
  8.3 9.3 %collective-permute-start.1 = (bf16[64,2048]{1,0:T(8,128)(2,1)S(1)}, bf16[64,2048]{1,0:T(8,128)(2,1)S(1)}, u32[]{:S(2)}, u32[]{:S(2)}) collective-permute-start(bf16[64,2048]{1,0:T(8,128)(2,1)S(1)} %constant_dynamic-slice_fusion.1), channel_id=1, source_target_pairs={{0,16},{4,20},{8,24},{12,28},{16,0},{20,4},{24,8},{28,12},{1,17},{... | collective-permute-start | bytes 786440 | tf_op jit(solution)/shard_map/ppermute | solution.py:11
  19.5 105.0 %all-gather.5.cloned.1.call-start = ((), (), s32[]{:S(2)}) async-start(), calls=%async_computation | async-start | bytes 4587520 | tf_op jit(solution)/shard_map/all_gather | solution.py:40
  19.5 16.2 %collective-permute-start = (bf16[128,2048]{1,0:T(8,128)(2,1)}, bf16[128,2048]{1,0:T(8,128)(2,1)S(1)}, u32[]{:S(2)}, u32[]{:S(2)}) collective-permute-start(bf16[128,2048]{1,0:T(8,128)(2,1)} %param.7), channel_id=1, source_target_pairs={{0,16},{4,20},{8,24},{12,28},{16,0},{20,4},{24,8},{28,12},{1,17},{... | collective-permute-start | bytes 1572872 | tf_op jit(solution)/shard_map/ppermute | solution.py:11
  22.4 1.2 copy-start.4
  23.7 12.1 %copy-start = (bf16[128,2048]{1,0:T(8,128)(2,1)S(1)}, bf16[128,2048]{1,0:T(8,128)(2,1)}, u32[]{:S(2)}) copy-start(bf16[128,2048]{1,0:T(8,128)(2,1)} %param.6) | copy-start | bytes 1572868
  23.7 12.0 %copy-start.3 = (bf16[128,2048]{1,0:T(8,128)(2,1)S(1)}, bf16[128,2048]{1,0:T(8,128)(2,1)}, u32[]{:S(2)}) copy-start(bf16[128,2048]{1,0:T(8,128)(2,1)} %param.7) | copy-start | bytes 1572868
Sparse Core Ops, SparseCore 0:
  19.6 31.1 all-gather.6
  52.4 72.1 all-gather.4
